TPU v7x, 1024 devices: a whole 4x8x16 slice. The times are simulated.
1024 devices in a mesh: blk: 32 (over z_hi, y), nbr: 32 (over z_lo, x, core).
Axes of the slice: x: 4, y: 8, z: 16 (z_hi: 4, z_lo: 4; z = z_hi * 4 + z_lo), core: 2. Of those that a mesh axis runs over, the one named last changes fastest.
Arguments:
- positions: float32 [3, 524288], P(None, ('blk', 'nbr')), may hold values from -6 to 6
- density: float32 [3, 524288], P(None, ('blk', 'nbr')), may hold values from -1.2 to 1.2
- upsample: float32 [32, 128], replicated, may hold values from -1 to 1
- cell_map: int32 [32, 32], P('blk'), may hold values from 0 to 31, as said below
- near_list: int32 [1024, 124, 2], P(('blk', 'nbr')), may hold values from -1 to 31, as said below
Outputs:
- velocity: float32 [3, 524288], P(None, ('blk', 'nbr'))
Inputs may be any that keep to these rules, and one draw needn't show every extreme that they name: Each row of cell_map is a permutation of the nbr indices. In near_list[c] every entry is either (-1, -1) or a pair (k, t) with t a cell id of c's row other than c's own; the pairs of one list are distinct; no cell id is named by more than 4 entries of one list, and in every row one cell is named by exactly 4 entries of every other cell's list.
All inputs are finite; a program needn't handle non-finite values.
Results may differ from a plain program's by a relative error of at most 0.0003.
Values sent between devices are 32-bit elements; how exact they have to be, the bound alone decides.
A program may use at most 32 MiB of HBM per device.

v0:
```python
import math

import jax
import jax.numpy as jnp
from jax import lax
from jax.sharding import PartitionSpec as P

FAR_REG_SQ = 0.0625
NEAR_REG_SQ = 0.01
STOKES_COEF = 1.0 / (8.0 * math.pi)


def stokeslet(targets, sources, densities, reg_sq):
    offset_vec = targets[:, :, None] - sources[:, None, :]
    dist_sq = jnp.sum(offset_vec * offset_vec, axis=0) + reg_sq
    inv_cube = lax.rsqrt(dist_sq) / dist_sq
    leading = (dist_sq + reg_sq) * inv_cube
    projected = jnp.sum(offset_vec * densities[:, None, :], axis=0) * inv_cube
    first = jnp.sum(leading[None] * densities[:, None, :], axis=-1)
    second = jnp.sum(offset_vec * projected[None], axis=-1)
    return STOKES_COEF * (first + second)


def upsample_panels(panel_data, table):
    raised = jnp.einsum("kcp,pw->kcw", panel_data, table, precision=lax.Precision.HIGHEST)
    ratio = panel_data.shape[2] / table.shape[1]
    return jnp.concatenate([raised[:, :3], raised[:, 3:] * ratio], axis=1)


def shards(positions, density, upsample, cell_map, near_list):
    points = positions.shape[1]
    panel_pts = upsample.shape[0]
    fine_pts = upsample.shape[1]
    panels = points // panel_pts
    peer_count = lax.axis_size("nbr")
    entries = near_list.shape[1]
    slot_count = entries // (peer_count - 1)
    own_block = jnp.concatenate([positions, density], axis=0)
    shard_piece = lax.all_gather(own_block, "blk", axis=1, tiled=True)
    block_count = shard_piece.shape[1] // points
    blocks = jnp.transpose(shard_piece.reshape(6, block_count, points), (1, 0, 2))

    def add_block(summed, source_block):
        return (summed + stokeslet(positions, source_block[:3], source_block[3:], FAR_REG_SQ), None)

    summed, _ = lax.scan(add_block, jnp.zeros((3, points), jnp.float32), blocks)
    far_field = summed
    coarse = jnp.transpose(own_block.reshape(6, panels, panel_pts), (1, 0, 2))
    panel_ids = near_list[0, :, 0]
    target_ids = near_list[0, :, 1]
    is_valid = target_ids >= 0
    row_map = cell_map[0]
    matches = target_ids[:, None] == jnp.arange(peer_count, dtype=jnp.int32)[None, :]
    dest_device = jnp.sum(jnp.where(matches, row_map[None, :], 0), axis=1)
    position = jnp.arange(entries, dtype=jnp.int32)
    earlier = (
        (dest_device[:, None] == dest_device[None, :])
        & is_valid[:, None]
        & is_valid[None, :]
        & (position[None, :] < position[:, None])
    )
    rank_in_dest = jnp.sum(earlier.astype(jnp.int32), axis=1)
    slot_id = dest_device * slot_count + rank_in_dest
    routing = (
        (jnp.arange(peer_count * slot_count, dtype=jnp.int32)[:, None] == slot_id[None, :])
        & is_valid[None, :]
    ).astype(jnp.float32)
    panel_pick = (panel_ids[:, None] == jnp.arange(panels, dtype=jnp.int32)[None, :]).astype(
        jnp.float32
    )
    picked = jnp.dot(routing, panel_pick, precision=lax.Precision.HIGHEST)
    fine_panels = upsample_panels(coarse, upsample).reshape(panels, 6 * fine_pts)
    outgoing = jnp.dot(picked, fine_panels, precision=lax.Precision.HIGHEST).reshape(
        peer_count, slot_count * 6 * fine_pts
    )
    incoming = lax.all_to_all(outgoing, "nbr", split_axis=0, concat_axis=0, tiled=True)
    sources = incoming.reshape(peer_count * slot_count, 6, fine_pts)
    group_size = 4
    block_width = group_size * fine_pts
    flattened = jnp.transpose(sources, (1, 0, 2)).reshape(6, peer_count * slot_count * fine_pts)
    near_blocks = jnp.transpose(
        flattened.reshape(6, peer_count * slot_count // group_size, block_width), (1, 0, 2)
    )

    def add_near(summed, source_block):
        return (
            summed + stokeslet(positions, source_block[:3], source_block[3:], NEAR_REG_SQ),
            None,
        )

    near_field, _ = lax.scan(add_near, jnp.zeros((3, points), jnp.float32), near_blocks)
    return far_field + near_field


def solution(mesh):
    placed = (
        P(None, ("blk", "nbr")),
        P(None, ("blk", "nbr")),
        P(),
        P("blk", None),
        P(("blk", "nbr"), None, None),
    )
    return jax.shard_map(
        shards, mesh=mesh, in_specs=placed, out_specs=P(None, ("blk", "nbr")), check_vma=False
    )
```

profile of v0, /device:TPU:2, one launch (start us, length us, event | category | flops | bytes accessed | tf_op | source)
XLA Modules:
  0.0 238.6 jit_solution(3991852604366616753)
XLA Ops:
  4.2 1.1 all_to_all.8
  5.3 16.7 %all-to-all-start = ((f32[32,1,3072]{2,1,0:T(1,128)}), f32[32,1,3072]{2,1,0:T(1,128)S(1)}, u32[]{:S(2)}, u32[]{:S(2)}) async-start(f32[32,1,3072]{2,1,0:T(1,128)} %all_to_all.8), calls=%async_computation | async-start | bytes 786432 | tf_op jit(solution)/shard_map/all_to_all | solution.py:76
  22.1 104.4 %all_gather.3 = f32[6,16384]{1,0:T(8,128)S(1)} all-gather(f32[6,512]{1,0:T(8,128)S(1)} %pad_maximum_fusion), channel_id=1, replica_groups=mesh['blk'=32,'nbr'=32] {'blk'}, dimensions={1}, use_global_device_ids=true | all-gather | bytes 405504 | tf_op jit(solution)/shard_map/all_gather | solution.py:39
  126.4 55.2 %while.26 = (s32[]{:T(128)}, f32[3,512]{1,0:T(4,128)S(1)}, f32[3,512]{1,0:T(4,128)S(1)}, f32[32,6,512]{2,1,0:T(8,128)S(1)}, s32[]{:T(128)}, /*index=5*/s32[]{:T(128)}, s32[]{}) while((s32[]{:T(128)}, f32[3,512]{1,0:T(4,128)S(1)}, f32[3,512]{1,0:T(4,128)S(1)}, f32[32,6,512]{2,1,0:T(8,128)S(1)}, s32[]{:T(128)}, /*index=5*/s32[]{:T(128)}, ...), condition=%wide.region_5.6_spmd.clone, body=%wide.region_0.5_spmd.clone.sunk | while | flops 8653828 | bytes 8487019 | solution.py:46
  127.3 0.8 fusion.31
  129.0 0.8 fusion.31
  135.9 0.8 fusion.31
  137.6 0.8 fusion.31
  139.4 0.8 fusion.31
  141.1 0.8 fusion.31
  148.0 0.8 fusion.31
  149.7 0.8 fusion.31
  151.4 0.8 fusion.31
  158.3 0.8 fusion.31
  160.1 0.8 fusion.31
  161.8 0.8 fusion.31
  168.7 0.8 fusion.31
  170.4 0.8 fusion.31
  172.1 0.8 fusion.31
  173.9 0.8 fusion.31
  180.8 0.8 fusion.31
  181.6 0.9 reduce
  182.8 55.2 %while.27 = (s32[]{:T(128)}, f32[3,512]{1,0:T(4,128)S(1)}, f32[3,512]{1,0:T(4,128)S(1)}, f32[32,6,512]{2,1,0:T(8,128)S(1)}, s32[]{:T(128)}, /*index=5*/s32[]{:T(128)}, s32[]{}) while((s32[]{:T(128)}, f32[3,512]{1,0:T(4,128)S(1)}, f32[3,512]{1,0:T(4,128)S(1)}, f32[32,6,512]{2,1,0:T(8,128)S(1)}, s32[]{:T(128)}, ...), condition=%wide.region_13.14_spmd.clone, body=%wide.region_8.13_spmd.clone.sunk | while | flops 8653828 | bytes 8487019 | solution.py:91
  183.7 0.8 fusion.34
  (322 shorter events, 97.7 us)
Async XLA Ops:
  0.0 3.2 %copy-start = (f32[32,128]{1,0:T(8,128)S(1)}, f32[32,128]{1,0:T(8,128)}, u32[]{:S(2)}) copy-start(f32[32,128]{1,0:T(8,128)} %param.11) | copy-start | bytes 49156
  4.2 122.3 %copy-start.1 = (f32[3,512]{1,0:T(4,128)S(1)}, f32[3,512]{1,0:T(4,128)}, u32[]{:S(2)}) copy-start(f32[3,512]{1,0:T(4,128)} %param.9) | copy-start | bytes 18436
  5.3 176.3 %all-to-all-start = ((f32[32,1,3072]{2,1,0:T(1,128)}), f32[32,1,3072]{2,1,0:T(1,128)S(1)}, u32[]{:S(2)}, u32[]{:S(2)}) async-start(f32[32,1,3072]{2,1,0:T(1,128)} %all_to_all.8), calls=%async_computation | async-start | bytes 786432 | tf_op jit(solution)/shard_map/all_to_all | solution.py:76
where the time goes:
time: 239 us
  other arithmetic  111 us (46%)
  blocking collectives  104 us (44%)
  starting transfers between devices  16.7 us (7%)
  local copies, waits for them, and re-layouts  2.92 us (1%)
  loops' own time  2.78 us (1%)
    all_gather x1, blocking collectives, shards(): shard_piece = lax.all_gather(own_block, 'blk', axis=1, tiled=True)  104 us
    reduce_sum x64, other arithmetic, stokeslet(): second = jnp.sum(offset_vec * projected[None], axis=-1)  52.7 us
    reduce_sum x64, other arithmetic, stokeslet(): projected = jnp.sum(offset_vec * densities[:, None, :], axis=0) * inv_cube  35.1 us
    mul x64, other arithmetic, stokeslet(): projected = jnp.sum(offset_vec * densities[:, None, :], axis=0) * inv_cube  18 us
    all_to_all x1, starting transfers between devices, shards(): lax.all_to_all(outgoing, 'nbr', split_axis=0, concat_axis=0, tiled=True)  16.7 us
  transfers between devices with their start and end apart: 1, of which 0 were waited for; matrix products, arithmetic and copies ran while one was open for 23% of the time, Pallas kernels for 0%

commit v1 on v0

v1 whole, which is shorter than its diff:
```python
import functools
import math

import jax
import jax.numpy as jnp
from jax import lax
from jax.experimental import pallas as pl
from jax.experimental.pallas import tpu as pltpu
from jax.sharding import PartitionSpec as P

F32 = jnp.float32
BF16 = jnp.bfloat16
MESH = pl.DeviceIdType.MESH
FAR_REG_SQ = 0.0625
NEAR_REG_SQ = 0.01
STOKES_COEF = 1.0 / (8.0 * math.pi)

PTS = 512
PEERS = 32
ZN = 4
YN = 8
NEAR_BLOCKS = PEERS - 1
FAR0 = NEAR_BLOCKS
BLOCKS = NEAR_BLOCKS + ZN * YN


def split3(a):
    a1 = a.astype(BF16)
    r = a - a1.astype(F32)
    a2 = r.astype(BF16)
    r = r - a2.astype(F32)
    return a1, a2, r.astype(BF16)


def split3f(a):
    a1 = a.astype(BF16).astype(F32)
    r = a - a1
    a2 = r.astype(BF16).astype(F32)
    return a1, a2, r - a2


def pack_kernel(list_ref, map_ref, pos_ref, den_ref, up_ref, own_ref, out_ref, wide_ref, table, count):
    zero = jnp.zeros((1, PTS), F32)
    own = jnp.concatenate([pos_ref[...], zero, den_ref[...], zero], axis=0)
    own_ref[...] = own
    row = lax.broadcasted_iota(jnp.int32, (8, 128), 0)
    scaled = [jnp.where(row < 4, own[:, 128 * v : 128 * v + 128], 0.25 * own[:, 128 * v : 128 * v + 128]) for v in range(4)]
    for v in range(4):
        for r in range(4):
            table[4 * v + r] = scaled[v] if r == 0 else pltpu.roll(scaled[v], 32 * r, 1)
    out_ref[...] = jnp.zeros_like(out_ref)
    up = up_ref[...]
    none = jnp.zeros_like(up)
    for s in range(4):
        wide_ref[32 * s : 32 * s + 32, :] = jnp.concatenate([up if q == s else none for q in range(4)], axis=1)
    lane_slot = lax.broadcasted_iota(jnp.int32, (8, 128), 1) // 32
    for j in range(PEERS + 1):
        count[j] = 0

    def entry(e, carry):
        k = jnp.maximum(list_ref[2 * e], 0)
        t = list_ref[2 * e + 1]
        dest = jnp.where(t >= 0, map_ref[0, jnp.maximum(t, 0)], PEERS)
        slot = jnp.bitwise_and(count[dest], 3)
        count[dest] = slot + 1
        tile = table[4 * (k // 4) + jnp.bitwise_and(slot - k, 3)]
        out_ref[dest] = jnp.where(lane_slot == slot, tile, out_ref[dest])
        return carry

    lax.fori_loop(0, list_ref.shape[0] // 2, entry, 0)


def bc(t, r):
    return jnp.broadcast_to(t[r : r + 1, :], t.shape)


def prepare(t, center, row, ya_ref, w_ref):
    tc = t - center
    g = pltpu.roll(tc, 4, 0)
    sq = tc * tc
    df = tc * g
    nb = jnp.broadcast_to(sq[0:1] + sq[1:2] + sq[2:3], t.shape)
    db = jnp.broadcast_to(df[0:1] + df[1:2] + df[2:3], t.shape)
    s = jnp.where(row < 3, tc, jnp.where(row == 3, nb, jnp.where(row == 4, 1.0, 0.0)))
    s1, s2, s3 = split3f(s)
    ya_ref[...] = jnp.concatenate([s1, s2, s3, s1, s2, s1], axis=0).astype(BF16)
    low = row < 4
    f2 = jnp.where(low, g, tc)
    w1 = jnp.where(low, bc(tc, 0), bc(tc, 1)) * f2
    w2 = jnp.where(low, bc(tc, 2) * g, nb * tc + db * g)
    w1 = jnp.where(row == 3, bc(tc, 4), jnp.where(row == 7, bc(tc, 5), w1))
    w2 = jnp.where(row == 3, bc(tc, 6), w2)
    p1, p2, p3 = split3(jnp.concatenate([w1, w2], axis=0))
    w_ref[0:16, :] = p1
    w_ref[16:32, :] = p2
    w_ref[32:48, :] = p3


def target_rows(x, reg_sq):
    n = x[0] * x[0] + x[1] * x[1] + x[2] * x[2]
    one = jnp.ones_like(n)
    z = jnp.zeros_like(n)
    t = jnp.concatenate([-2.0 * x[0], -2.0 * x[1], -2.0 * x[2], one, n + reg_sq, z, z, z], axis=0)
    t1, t2, t3 = split3f(t)
    return jnp.concatenate([t1, t1, t1, t2, t2, t3], axis=0).astype(BF16), n


def weights(ya_ref, xa, hi_ref, lo_ref):
    d = lax.dot_general(ya_ref[...], xa, (((0,), (0,)), ((), ())), preferred_element_type=F32)
    s = lax.rsqrt(d)
    b = s * (s * s)
    hi = b.astype(BF16)
    hi_ref[...] = hi
    lo_ref[...] = (b - hi.astype(F32)).astype(BF16)


def contract(w_ref, hi_ref, lo_ref):
    p = jnp.dot(w_ref[...], hi_ref[...], preferred_element_type=F32)
    q = jnp.dot(w_ref[0:32, :], lo_ref[...], preferred_element_type=F32)
    return p[:16] + p[16:32] + p[32:] + q[:16] + q[16:]


def combine(acc, x, n, reg_sq):
    f = [acc[3:4], acc[7:8], acc[11:12]]
    yf = [[acc[4 * b + a : 4 * b + a + 1] for a in range(3)] for b in range(3)]
    z = [acc[12 + a : 13 + a] for a in range(3)]
    xf = x[0] * f[0] + x[1] * f[1] + x[2] * f[2] - (yf[0][0] + yf[1][1] + yf[2][2])
    out = []
    for a in range(3):
        t = (2 * reg_sq + n) * f[a] + z[a]
        for b in range(3):
            t = t - x[b] * (2.0 * yf[b][a] + yf[a][b])
        out.append(t + x[a] * xf)
    return out


def main_kernel(
    own_ref, tiles_ref, wide_ref, out_ref,
    big, coarse, xa_ref, acc_ref, ya0, ya1, w0, w1, hi0, hi1, lo0, lo1,
    near_send, near_recv, far_send, far_recv,
):
    blk = lax.axis_index("blk")
    nbr = lax.axis_index("nbr")
    zh = blk // YN
    y = lax.rem(blk, YN)

    def column(dz, dy):
        return (lax.rem(zh + dz, ZN) * YN + lax.rem(y + dy, YN), nbr)

    def row_peer(o):
        return (blk, lax.rem(nbr + o, PEERS))

    def far_copy(src, dz, dy, hop_z, hop_y):
        f = dz * YN + dy
        return pltpu.make_async_remote_copy(
            src_ref=src, dst_ref=big.at[FAR0 + f], send_sem=far_send.at[f], recv_sem=far_recv.at[f],
            device_id=column(hop_z, hop_y), device_id_type=MESH,
        )

    def near_copy(o):
        return pltpu.make_async_remote_copy(
            src_ref=tiles_ref.at[lax.rem(nbr + o, PEERS)], dst_ref=coarse.at[o - 1],
            send_sem=near_send.at[o - 1], recv_sem=near_recv.at[o - 1],
            device_id=row_peer(o), device_id_type=MESH,
        )

    barrier = pltpu.get_barrier_semaphore()
    for dz in (1, ZN - 1):
        pl.semaphore_signal(barrier, inc=1, device_id=column(dz, 0), device_id_type=MESH)

    def greet_row(o, c):
        pl.semaphore_signal(barrier, inc=1, device_id=row_peer(o), device_id_type=MESH)
        return c

    def greet_column(o, c):
        pl.semaphore_signal(barrier, inc=1, device_id=column(0, o), device_id_type=MESH)
        return c

    lax.fori_loop(1, YN, greet_column, 0)
    lax.fori_loop(1, PEERS, greet_row, 0)

    own = own_ref[...]
    big[FAR0] = own
    zero = jnp.zeros((1, 1), F32)
    means = [jnp.mean(own[i : i + 1], axis=1, keepdims=True) for i in range(3)]
    center = jnp.concatenate(means + [zero] * 5, axis=0)
    x = [own[i : i + 1] - means[i] for i in range(3)]
    xa_ref[0], n = target_rows(x, NEAR_REG_SQ)
    xa_ref[1], _ = target_rows(x, FAR_REG_SQ)
    acc_ref[...] = jnp.zeros_like(acc_ref)
    row = lax.broadcasted_iota(jnp.int32, (8, PTS), 0)
    u1, u2, u3 = split3(wide_ref[...])

    pl.semaphore_wait(barrier, 2 + (YN - 1) + (PEERS - 1))
    far_copy(own_ref, 1, 0, 1, 0).start()
    far_copy(own_ref, 3, 0, 3, 0).start()

    def send_near(o, c):
        near_copy(o).start()
        return c

    def send_own(o, c):
        far_copy(own_ref, 0, o, 0, o).start()
        return c

    def fan(dz):
        def send(o, c):
            far_copy(big.at[FAR0 + dz * YN], dz, o, 0, o).start()
            return c

        return send

    lax.fori_loop(1, PEERS, send_near, 0)
    lax.fori_loop(1, YN, send_own, 0)

    def take_near(o, c):
        near_copy(o).wait_recv()
        return c

    lax.fori_loop(1, PEERS, take_near, 0)
    far_copy(own_ref, 1, 0, 1, 0).wait_recv()
    far_copy(big.at[FAR0 + YN], 2, 0, 1, 0).start()
    lax.fori_loop(1, YN, fan(1), 0)
    far_copy(own_ref, 3, 0, 3, 0).wait_recv()
    lax.fori_loop(1, YN, fan(3), 0)

    a1, a2, a3 = split3(coarse[...].reshape(NEAR_BLOCKS * 8, 128))
    dot = functools.partial(jnp.dot, preferred_element_type=F32)
    fine = dot(a1, u1) + (dot(a1, u2) + dot(a2, u1)) + (dot(a1, u3) + dot(a2, u2) + dot(a3, u1))
    big[0:NEAR_BLOCKS] = fine.reshape(NEAR_BLOCKS, 8, PTS)

    ya = (ya0, ya1)
    w = (w0, w1)
    hi = (hi0, hi1)
    lo = (lo0, lo1)

    def kind(i):
        return jnp.where(i < FAR0, 0, 1)

    def step(i, p, first=False, last=False):
        q = 1 - p
        if not first:
            s = kind(i - 1)
            acc_ref[s] += contract(w[q], hi[q], lo[q])
        weights(ya[p], xa_ref[kind(i)], hi[p], lo[p])
        if not last:
            prepare(big[i + 1], center, row, ya[q], w[q])

    def take_far(f):
        @pl.when(lax.rem(f, YN) != 0)
        def _():
            far_copy(own_ref, 0, f, 0, 1).wait_recv()

    def pair(k, c):
        step(2 * k + 1, 1)
        step(2 * k + 2, 0)
        return c

    def far_pair(k, c):
        take_far(2 * k + 2 - FAR0)
        take_far(2 * k + 3 - FAR0)
        return pair(k, c)

    prepare(big[0], center, row, ya0, w0)
    step(0, 0, first=True)
    lax.fori_loop(0, 4, pair, 0)
    far_copy(big.at[FAR0 + YN], 2, 0, 1, 0).wait_recv()
    lax.fori_loop(1, YN, fan(2), 0)
    lax.fori_loop(4, 15, pair, 0)
    lax.fori_loop(15, 30, far_pair, 0)
    take_far(BLOCKS - 1 - FAR0)
    step(BLOCKS - 2, 1)
    step(BLOCKS - 1, 0, last=True)
    acc_ref[1] += contract(w0, hi0, lo0)

    near = combine(acc_ref[0], x, n, NEAR_REG_SQ)
    far = combine(acc_ref[1], x, n, FAR_REG_SQ)
    for a in range(3):
        out_ref[a : a + 1, :] = STOKES_COEF * (far[a] + near[a])

    def sent_near(o, c):
        near_copy(o).wait_send()
        return c

    def sent_far(f, c):
        far_copy(own_ref, 0, f, 0, 1).wait_send()
        return c

    lax.fori_loop(1, PEERS, sent_near, 0)
    lax.fori_loop(1, ZN * YN, sent_far, 0)


def shards(positions, density, upsample, cell_map, near_list):
    vmem = pl.BlockSpec(memory_space=pltpu.VMEM)
    smem = pl.BlockSpec(memory_space=pltpu.SMEM)
    own, tiles, wide = pl.pallas_call(
        pack_kernel,
        out_shape=(
            jax.ShapeDtypeStruct((8, PTS), F32),
            jax.ShapeDtypeStruct((PEERS + 1, 8, 128), F32),
            jax.ShapeDtypeStruct((128, PTS), F32),
        ),
        in_specs=[smem, smem, vmem, vmem, vmem],
        out_specs=(vmem, vmem, vmem),
        scratch_shapes=[pltpu.VMEM((16, 8, 128), F32), pltpu.SMEM((PEERS + 1,), jnp.int32)],
    )(near_list.reshape(-1), cell_map, positions, density, upsample)
    return pl.pallas_call(
        main_kernel,
        out_shape=jax.ShapeDtypeStruct((3, PTS), F32),
        in_specs=[vmem, vmem, vmem],
        out_specs=vmem,
        scratch_shapes=[
            pltpu.VMEM((BLOCKS, 8, PTS), F32),
            pltpu.VMEM((NEAR_BLOCKS, 8, 128), F32),
            pltpu.VMEM((2, 48, PTS), BF16),
            pltpu.VMEM((2, 16, PTS), F32),
        ]
        + [pltpu.VMEM((48, PTS), BF16)] * 4
        + [pltpu.VMEM((PTS, PTS), BF16)] * 4
        + [pltpu.SemaphoreType.DMA((NEAR_BLOCKS,))] * 2
        + [pltpu.SemaphoreType.DMA((ZN * YN,))] * 2,
        compiler_params=pltpu.CompilerParams(
            collective_id=0, has_side_effects=True, vmem_limit_bytes=48 << 20
        ),
    )(own, tiles, wide)


def solution(mesh):
    placed = (
        P(None, ("blk", "nbr")),
        P(None, ("blk", "nbr")),
        P(),
        P("blk", None),
        P(("blk", "nbr"), None, None),
    )
    return jax.shard_map(
        shards, mesh=mesh, in_specs=placed, out_specs=P(None, ("blk", "nbr")), check_vma=False
    )
```

time: 239 us -> 72.8 us (0.30)
  the two profiles are of different devices: /device:TPU:2 before, /device:TPU:1 now
where the time goes in v1:
time: 72.8 us; the launch traced here: 72.5 us
  Pallas kernels  67.8 us (93%)
  local copies, waits for them, and re-layouts  4.67 us (6%)
    pallas_call x1, Pallas kernels, shards(): pl.pallas_call(main_kernel, out_shape=jax.ShapeDtypeStruct((3, PTS), F32)...  63.9 us
    unnamed x8, local copies, waits for them, and re-layouts  3.97 us
    pallas_call x1, Pallas kernels, shards(): pl.pallas_call(pack_kernel, out_shape=(jax.ShapeDtypeStruct((8, PTS), F32...  3.9 us

profile of v1, /device:TPU:1, one launch (start us, length us, event | category | flops | bytes accessed | tf_op | source)
XLA Modules:
  0.0 72.5 jit_solution(3909738659820548222)
XLA Ops:
  0.0 0.8 %copy.6 = s32[1,124,2]{2,1,0:T(8,128)S(1)} copy(s32[1,124,2]{1,2,0:T(2,128)} %param.9) | data formatting | bytes 1984 | tf_op args[4]
  0.8 0.7 reshape.3.list_ref
  1.5 3.9 %shard_map.55 = (f32[8,512]{1,0:T(8,128)}, f32[33,8,128]{2,1,0:T(8,128)}, f32[128,512]{1,0:T(8,128)}) custom-call(s32[248]{0:T(256)} %reshape.3.list_ref, s32[1,32]{1,0:T(1,128)} %map_ref.1, f32[3,512]{1,0:T(4,128)} %pos_ref.1, f32[3,512]{1,0:T(4,128)} %den_ref.1, f32[32,128]{1,0:T(8,128)} %up_ref.1), custom_call_target="tpu_custom_call" | custom-call | tf_op jit(solution)/shard_map/pallas_call | solution.py:296
  5.4 0.0 copy-start
  5.4 0.9 %copy-done = f32[128,512]{1,0:T(8,128)S(1)} copy-done((f32[128,512]{1,0:T(8,128)S(1)}, f32[128,512]{1,0:T(8,128)}, u32[]{:S(2)}) %copy-start) | copy-done | bytes 262168
  6.4 0.0 copy-start.1
  6.4 0.9 %copy-done.1 = f32[33,8,128]{2,1,0:T(8,128)S(1)} copy-done((f32[33,8,128]{2,1,0:T(8,128)S(1)}, f32[33,8,128]{2,1,0:T(8,128)}, u32[]{:S(2)}) %copy-start.1) | copy-done | bytes 135192
  7.3 0.0 copy-start.2
  7.3 0.7 copy-done.2
  8.0 63.9 %shard_map.56 = f32[3,512]{1,0:T(4,128)S(1)} custom-call(f32[8,512]{1,0:T(8,128)S(1)} %copy-done.2, f32[33,8,128]{2,1,0:T(8,128)S(1)} %copy-done.1, f32[128,512]{1,0:T(8,128)S(1)} %copy-done), custom_call_target="tpu_custom_call" | custom-call | tf_op jit(solution)/shard_map/pallas_call | solution.py:307
  71.9 0.6 copy.8
Async XLA Ops:
  5.4 0.9 %copy-start = (f32[128,512]{1,0:T(8,128)S(1)}, f32[128,512]{1,0:T(8,128)}, u32[]{:S(2)}) copy-start(f32[128,512]{1,0:T(8,128)} %get-tuple-element.10.wide_ref) | copy-start | bytes 786436
  6.4 0.9 %copy-start.1 = (f32[33,8,128]{2,1,0:T(8,128)S(1)}, f32[33,8,128]{2,1,0:T(8,128)}, u32[]{:S(2)}) copy-start(f32[33,8,128]{2,1,0:T(8,128)} %get-tuple-element.9.tiles_ref) | copy-start | bytes 405508
  7.3 0.7 copy-start.2

commit v2 on v1

v2 whole, which is shorter than its diff:
```python
import functools
import math

import jax
import jax.numpy as jnp
from jax import lax
from jax.experimental import pallas as pl
from jax.experimental.pallas import tpu as pltpu
from jax.sharding import PartitionSpec as P

F32 = jnp.float32
BF16 = jnp.bfloat16
MESH = pl.DeviceIdType.MESH
FAR_REG_SQ = 0.0625
NEAR_REG_SQ = 0.01
STOKES_COEF = 1.0 / (8.0 * math.pi)

PTS = 512
PANELS = 16
SLOTS = 4
PEERS = 32
ZN = 4
YN = 8
XN = 4
NEAR_FIRST = 8
COLUMN = ZN * YN
FAR0 = PEERS - 1
BLOCKS = FAR0 + COLUMN
CHUNK = 64


def split3(a):
    a1 = a.astype(BF16)
    r = a - a1.astype(F32)
    a2 = r.astype(BF16)
    r = r - a2.astype(F32)
    return a1, a2, r.astype(BF16)


def split3f(a):
    a1 = a.astype(BF16).astype(F32)
    r = a - a1
    a2 = r.astype(BF16).astype(F32)
    return a1, a2, r - a2


def bc(t, r):
    return jnp.broadcast_to(t[r : r + 1, :], t.shape)


def prepare(t, center, row, ya_ref, w_ref):
    tc = t - center
    g = pltpu.roll(tc, 4, 0)
    sq = tc * tc
    df = tc * g
    nb = jnp.broadcast_to(sq[0:1] + sq[1:2] + sq[2:3], t.shape)
    db = jnp.broadcast_to(df[0:1] + df[1:2] + df[2:3], t.shape)
    s = jnp.where(row < 3, tc, jnp.where(row == 3, nb, jnp.where(row == 4, 1.0, 0.0)))
    s1, s2, s3 = split3f(s)
    ya_ref[...] = jnp.concatenate([s1, s2, s3, s1, s2, s1], axis=0).astype(BF16)
    low = row < 4
    f2 = jnp.where(low, g, tc)
    w1 = jnp.where(low, bc(tc, 0), bc(tc, 1)) * f2
    w2 = jnp.where(low, bc(tc, 2) * g, nb * tc + db * g)
    w1 = jnp.where(row == 3, bc(tc, 4), jnp.where(row == 7, bc(tc, 5), w1))
    w2 = jnp.where(row == 3, bc(tc, 6), w2)
    p1, p2, p3 = split3(jnp.concatenate([w1, w2], axis=0))
    for o in (0, PTS):
        w_ref[0:16, o : o + PTS] = p1
        w_ref[16:32, o : o + PTS] = p2
        w_ref[32:48, o : o + PTS] = p3


def target_rows(x, reg_sq):
    n = x[0] * x[0] + x[1] * x[1] + x[2] * x[2]
    one = jnp.ones_like(n)
    z = jnp.zeros_like(n)
    t = jnp.concatenate([-2.0 * x[0], -2.0 * x[1], -2.0 * x[2], one, n + reg_sq, z, z, z], axis=0)
    t1, t2, t3 = split3f(t)
    return jnp.concatenate([t1, t1, t1, t2, t2, t3], axis=0).astype(BF16), n


def distances(ya_ref, r, n, xa, d_ref):
    d_ref[r : r + n, :] = lax.dot_general(
        ya_ref[:, r : r + n], xa, (((0,), (0,)), ((), ())), preferred_element_type=F32
    )


def weights(d_ref, r, n, b_ref):
    s = lax.rsqrt(d_ref[r : r + n, :])
    b = s * (s * s)
    hi = b.astype(BF16)
    b_ref[r : r + n, :] = hi
    b_ref[PTS + r : PTS + r + n, :] = (b - hi.astype(F32)).astype(BF16)


def contract(w_ref, b_ref):
    p = jnp.dot(w_ref[...], b_ref[...], preferred_element_type=F32)
    return p[:16] + p[16:32] + p[32:]


def combine(acc, x, n, reg_sq):
    f = [acc[3:4], acc[7:8], acc[11:12]]
    yf = [[acc[4 * b + a : 4 * b + a + 1] for a in range(3)] for b in range(3)]
    z = [acc[12 + a : 13 + a] for a in range(3)]
    xf = x[0] * f[0] + x[1] * f[1] + x[2] * f[2] - (yf[0][0] + yf[1][1] + yf[2][2])
    out = []
    for a in range(3):
        t = (2 * reg_sq + n) * f[a] + z[a]
        for b in range(3):
            t = t - x[b] * (2.0 * yf[b][a] + yf[a][b])
        out.append(t + x[a] * xf)
    return out


def upsampled(tiles, up):
    a1, a2, a3 = split3(tiles.reshape(-1, 128))
    u1, u2, u3 = up
    dot = functools.partial(jnp.dot, preferred_element_type=F32)
    fine = dot(a1, u1) + (dot(a1, u2) + dot(a2, u1)) + (dot(a1, u3) + dot(a2, u2) + dot(a3, u1))
    return fine.reshape(-1, 8, PTS)


def main_kernel(
    pos_hbm, den_hbm, up_hbm, map_hbm, list_hbm, out_ref,
    pos_ref, den_ref, up_ref, map_ref, list_ref, ids_ref, ids_smem, table, tiles, wide,
    own_ref, coarse, big, xa_ref, acc_ref, ya0, ya1, w0, w1, w2, w3, d0, d1, b0, b1,
    load_sem, near_send, near_recv, far_send, far_recv,
):
    blk = lax.axis_index("blk")
    nbr = lax.axis_index("nbr")
    zh = blk // YN
    y = lax.rem(blk, YN)
    zl = nbr // (2 * XN)
    xc = lax.rem(nbr // 2, XN)
    core = lax.rem(nbr, 2)

    def column(dz, dy):
        return (lax.rem(zh + dz, ZN) * YN + lax.rem(y + dy, YN), nbr)

    def row_index(o):
        dz = o // (2 * XN)
        dx = lax.rem(o // 2, XN)
        dc = lax.rem(o, 2)
        return (lax.rem(zl + dz, ZN) * XN + lax.rem(xc + dx, XN)) * 2 + lax.rem(core + dc, 2)

    def far_copy(src, dz, dy, hop_z, hop_y):
        f = dz * YN + dy
        return pltpu.make_async_remote_copy(
            src_ref=src, dst_ref=big.at[FAR0 + f], send_sem=far_send.at[f], recv_sem=far_recv.at[f],
            device_id=column(hop_z, hop_y), device_id_type=MESH,
        )

    def near_copy(o):
        return pltpu.make_async_remote_copy(
            src_ref=tiles.at[o], dst_ref=coarse.at[o - 1],
            send_sem=near_send.at[o - 1], recv_sem=near_recv.at[o - 1],
            device_id=(blk, row_index(o)), device_id_type=MESH,
        )

    loads = [
        pltpu.make_async_copy(src, dst, load_sem.at[q])
        for q, (src, dst) in enumerate(
            ((list_hbm, list_ref), (map_hbm, map_ref), (pos_hbm, pos_ref), (den_hbm, den_ref), (up_hbm, up_ref))
        )
    ]
    for load in loads:
        load.start()
    barrier = pltpu.get_barrier_semaphore()
    for dz in (1, ZN - 1):
        pl.semaphore_signal(barrier, inc=1, device_id=column(dz, 0), device_id_type=MESH)

    def greet_row(o, c):
        pl.semaphore_signal(barrier, inc=1, device_id=(blk, row_index(PEERS - o)), device_id_type=MESH)
        return c

    def greet_column(o, c):
        pl.semaphore_signal(barrier, inc=1, device_id=column(0, o), device_id_type=MESH)
        return c

    lax.fori_loop(1, PEERS, greet_row, 0)
    lax.fori_loop(1, YN, greet_column, 0)
    for load in loads:
        load.wait()

    peer_row = lax.broadcasted_iota(jnp.int32, (PEERS, PEERS), 0)
    place = jnp.where(peer_row == map_ref[...], 1.0, 0.0).astype(BF16)
    entries = list_ref.shape[1]
    ids = list_ref[...]
    panel = ids[0:1, :]
    target = ids[1:2, :]
    cell = lax.broadcasted_iota(jnp.int32, (PEERS, entries), 0)
    named = jnp.where(cell == target, 1.0, 0.0).astype(BF16)
    hit = jnp.dot(place, named, preferred_element_type=F32)
    before = jnp.where(
        lax.broadcasted_iota(jnp.int32, (entries, entries), 0) < lax.broadcasted_iota(jnp.int32, (entries, entries), 1),
        1.0, 0.0,
    ).astype(BF16)
    rank = jnp.dot(hit.astype(BF16), before, preferred_element_type=F32)
    number = (panel + 1).astype(F32)
    lane = lax.broadcasted_iota(jnp.int32, (PEERS, 128), 1)
    chosen = jnp.zeros((PEERS, 128), F32)
    for s in range(SLOTS):
        value = jnp.sum(jnp.where((hit > 0.5) & (rank == s), number, 0.0), axis=1, keepdims=True)
        chosen = jnp.where(lane == s, value, chosen)
    ids_ref[...] = chosen.astype(jnp.int32)
    to_smem = pltpu.make_async_copy(ids_ref, ids_smem, load_sem.at[0])
    to_smem.start()

    zero = jnp.zeros((1, PTS), F32)
    own = jnp.concatenate([pos_ref[...], zero, den_ref[...], zero], axis=0)
    own_ref[...] = own
    big[FAR0] = own
    upper = lax.broadcasted_iota(jnp.int32, (8, 128), 0) < 4
    for v in range(4):
        part = own[:, 128 * v : 128 * v + 128]
        part = jnp.where(upper, part, 0.25 * part)
        for r in range(4):
            table[4 * v + r] = part if r == 0 else pltpu.roll(part, 32 * r, 1)
    table[PANELS] = jnp.zeros((8, 128), F32)
    lane_slot = lax.broadcasted_iota(jnp.int32, (8, 128), 1) // 32
    to_smem.wait()

    def route(o, c):
        peer = row_index(o)
        tile = jnp.zeros((8, 128), F32)
        for s in range(SLOTS):
            k = jnp.minimum(jnp.maximum(ids_smem[peer, s] - 1, -1), PANELS - 1)
            at = jnp.where(k < 0, PANELS, 4 * (k // 4) + jnp.bitwise_and(s - k, 3))
            at = jnp.minimum(jnp.maximum(at, 0), PANELS)
            tile = jnp.where(lane_slot == s, table[at], tile)
        tiles[o] = tile
        return c

    lax.fori_loop(1, PEERS, route, 0)

    up = up_ref[...]
    none = jnp.zeros_like(up)
    for s in range(SLOTS):
        wide[32 * s : 32 * s + 32, :] = jnp.concatenate([up if q == s else none for q in range(SLOTS)], axis=1)
    z1 = jnp.zeros((1, 1), F32)
    means = [jnp.mean(own[i : i + 1], axis=1, keepdims=True) for i in range(3)]
    center = jnp.concatenate(means + [z1] * 5, axis=0)
    x = [own[i : i + 1] - means[i] for i in range(3)]
    xa_ref[0], n = target_rows(x, NEAR_REG_SQ)
    xa_ref[1], _ = target_rows(x, FAR_REG_SQ)
    acc_ref[...] = jnp.zeros_like(acc_ref)
    b1[...] = jnp.zeros_like(b1)
    w3[...] = jnp.zeros_like(w3)
    row = lax.broadcasted_iota(jnp.int32, (8, PTS), 0)

    pl.semaphore_wait(barrier, 2 + (YN - 1) + (PEERS - 1))
    far_copy(own_ref, 1, 0, 1, 0).start()
    far_copy(own_ref, 3, 0, 3, 0).start()

    def send_near(o, c):
        near_copy(o).start()
        return c

    def send_own(o, c):
        far_copy(own_ref, 0, o, 0, o).start()
        return c

    def take_near(o, c):
        near_copy(o).wait_recv()
        return c

    def fan(dz):
        def send(o, c):
            far_copy(big.at[FAR0 + dz * YN], dz, o, 0, o).start()
            return c

        return send

    lax.fori_loop(1, PEERS, send_near, 0)
    lax.fori_loop(1, YN, send_own, 0)

    ya = (ya0, ya1)
    w = (w0, w1, w2, w3)
    d = (d0, d1)
    b = (b0, b1)

    def block(i):
        return jnp.where(i == 0, FAR0, jnp.where(i < PEERS, i - 1, i))

    def kind(i):
        return jnp.where(i == 0, 1, jnp.where(i < PEERS, 0, 1))

    def prep(i, j):
        prepare(big[block(i)], center, row, ya[j % 2], w[j % 4])

    def step(i, j, more=2):
        p = j % 2
        q = 1 - p
        half = PTS // 2
        xa = xa_ref[kind(i + 1)]
        if more > 0:
            distances(ya[q], 0, half, xa, d[q])
        acc_ref[kind(i - 1)] += contract(w[(j - 1) % 4], b[q])
        for r in range(4):
            weights(d[p], CHUNK * r, CHUNK, b[p])
        if more > 0:
            distances(ya[q], half, half, xa, d[q])
        for r in range(4, 8):
            weights(d[p], CHUNK * r, CHUNK, b[p])
        if more > 1:
            prep(i + 2, j + 2)

    prep(0, 0)
    distances(ya0, 0, PTS, xa_ref[1], d0)
    lax.fori_loop(1, NEAR_FIRST, take_near, 0)
    fine = functools.partial(upsampled, up=split3(wide[...]))
    big[0 : NEAR_FIRST - 1] = fine(coarse[0 : NEAR_FIRST - 1])
    prep(1, 1)

    def take_far(f):
        @pl.when((f > 0) & (lax.rem(f, YN) != 0))
        def _():
            far_copy(own_ref, 0, f, 0, 1).wait_recv()

    def body(k, c):
        @pl.when(k == 1)
        def _():
            far_copy(own_ref, 1, 0, 1, 0).wait_recv()
            far_copy(big.at[FAR0 + YN], 2, 0, 1, 0).start()
            lax.fori_loop(1, YN, fan(1), 0)
            far_copy(own_ref, 3, 0, 3, 0).wait_recv()
            lax.fori_loop(1, YN, fan(3), 0)
            lax.fori_loop(NEAR_FIRST, PEERS, take_near, 0)
            big[NEAR_FIRST - 1 : FAR0] = fine(coarse[NEAR_FIRST - 1 : FAR0])

        @pl.when(k == 3)
        def _():
            far_copy(big.at[FAR0 + YN], 2, 0, 1, 0).wait_recv()
            lax.fori_loop(1, YN, fan(2), 0)

        for j in range(4):
            take_far(4 * k + j + 2 - FAR0)
        for j in range(4):
            step(4 * k + j, j)
        return c

    lax.fori_loop(0, 15, body, 0)
    take_far(BLOCKS - 1 - FAR0)
    step(BLOCKS - 3, 0)
    step(BLOCKS - 2, 1, more=1)
    step(BLOCKS - 1, 2, more=0)
    acc_ref[1] += contract(w2, b0)

    near = combine(acc_ref[0], x, n, NEAR_REG_SQ)
    far = combine(acc_ref[1], x, n, FAR_REG_SQ)
    for a in range(3):
        out_ref[a : a + 1, :] = STOKES_COEF * (far[a] + near[a])

    def sent_near(o, c):
        near_copy(o).wait_send()
        return c

    def sent_far(f, c):
        far_copy(own_ref, 0, f, 0, 1).wait_send()
        return c

    lax.fori_loop(1, PEERS, sent_near, 0)
    lax.fori_loop(1, COLUMN, sent_far, 0)


def shards(positions, density, upsample, cell_map, near_list):
    entries = near_list.shape[1]
    anywhere = pl.BlockSpec(memory_space=pl.ANY)
    return pl.pallas_call(
        main_kernel,
        out_shape=jax.ShapeDtypeStruct((3, PTS), F32),
        in_specs=[anywhere] * 5,
        out_specs=pl.BlockSpec(memory_space=pltpu.VMEM),
        scratch_shapes=[
            pltpu.VMEM((3, PTS), F32),
            pltpu.VMEM((3, PTS), F32),
            pltpu.VMEM(upsample.shape, F32),
            pltpu.VMEM((1, PEERS), jnp.int32),
            pltpu.VMEM((2, entries), jnp.int32),
            pltpu.VMEM((PEERS, 128), jnp.int32),
            pltpu.SMEM((PEERS, 128), jnp.int32),
            pltpu.VMEM((PANELS + 1, 8, 128), F32),
            pltpu.VMEM((PEERS, 8, 128), F32),
            pltpu.VMEM((128, PTS), F32),
            pltpu.VMEM((8, PTS), F32),
            pltpu.VMEM((PEERS - 1, 8, 128), F32),
            pltpu.VMEM((BLOCKS, 8, PTS), F32),
            pltpu.VMEM((2, 48, PTS), BF16),
            pltpu.VMEM((2, 16, PTS), F32),
        ]
        + [pltpu.VMEM((48, PTS), BF16)] * 2
        + [pltpu.VMEM((48, 2 * PTS), BF16)] * 4
        + [pltpu.VMEM((PTS, PTS), F32)] * 2
        + [pltpu.VMEM((2 * PTS, PTS), BF16)] * 2
        + [pltpu.SemaphoreType.DMA((5,))]
        + [pltpu.SemaphoreType.DMA((PEERS - 1,))] * 2
        + [pltpu.SemaphoreType.DMA((COLUMN,))] * 2,
        compiler_params=pltpu.CompilerParams(
            collective_id=0, has_side_effects=True, vmem_limit_bytes=62 << 20
        ),
    )(positions, density, upsample, cell_map, jnp.transpose(near_list, (0, 2, 1)).reshape(2, entries))


def solution(mesh):
    placed = (
        P(None, ("blk", "nbr")),
        P(None, ("blk", "nbr")),
        P(),
        P("blk", None),
        P(("blk", "nbr"), None, None),
    )
    return jax.shard_map(
        shards, mesh=mesh, in_specs=placed, out_specs=P(None, ("blk", "nbr")), check_vma=False
    )
```

time: 72.8 us -> 58.4 us (0.80)
  Pallas kernels: 67.8 us -> 57 us
  local copies, waits for them, and re-layouts: 4.67 us -> 1.3 us
    pallas_call x1, Pallas kernels: 63.9 us -> 57 us  [shards(): pl.pallas_call(main_kernel, out_shape=jax.ShapeDtypeStruct((3, PTS), F32)...]
    pallas_call x1 -> x0, Pallas kernels: 3.9 us -> none  [shards(): pl.pallas_call(pack_kernel, out_shape=(jax.ShapeDtypeStruct((8, PTS), F32...]
    unnamed x8 -> x1, local copies, waits for them, and re-layouts: 3.97 us -> 1.3 us
where the time goes in v2:
time: 58.4 us; the launch traced here: 58.3 us
  Pallas kernels  57 us (98%)
  local copies, waits for them, and re-layouts  1.3 us (2%)
    pallas_call x1, Pallas kernels, shards(): pl.pallas_call(main_kernel, out_shape=jax.ShapeDtypeStruct((3, PTS), F32)...  57 us
    unnamed x1, local copies, waits for them, and re-layouts  1.3 us

profile of v2, /device:TPU:1, one launch (start us, length us, event | category | flops | bytes accessed | tf_op | source)
XLA Modules:
  0.0 58.3 jit_solution(3964997526042307769)
XLA Ops:
  0.0 57.0 %shard_map.55 = f32[3,512]{1,0:T(4,128)} custom-call(f32[3,512]{1,0:T(4,128)} %pos_hbm.1, f32[3,512]{1,0:T(4,128)} %den_hbm.1, f32[32,128]{1,0:T(8,128)} %up_hbm.1, s32[1,32]{1,0:T(1,128)} %map_hbm.1, s32[2,124]{1,0:T(2,128)} %bitcast.3), custom_call_target="tpu_custom_call" | custom-call | tf_op jit(solution)/shard_map/pallas_call | solution.py:370
  57.0 1.3 %copy.7 = f32[3,512]{1,0:T(4,128)} copy(f32[3,512]{1,0:T(4,128)} %shard_map.55) | data formatting | bytes 12288

commit v3 on v2

--- a/solution.py
+++ b/solution.py
@@ -65,10 +65,9 @@
     w1 = jnp.where(row == 3, bc(tc, 4), jnp.where(row == 7, bc(tc, 5), w1))
     w2 = jnp.where(row == 3, bc(tc, 6), w2)
     p1, p2, p3 = split3(jnp.concatenate([w1, w2], axis=0))
-    for o in (0, PTS):
-        w_ref[0:16, o : o + PTS] = p1
-        w_ref[16:32, o : o + PTS] = p2
-        w_ref[32:48, o : o + PTS] = p3
+    w_ref[0:16, :] = p1
+    w_ref[16:32, :] = p2
+    w_ref[32:48, :] = p3
 
 
 def target_rows(x, reg_sq):
@@ -94,9 +93,14 @@
     b_ref[PTS + r : PTS + r + n, :] = (b - hi.astype(F32)).astype(BF16)
 
 
-def contract(w_ref, b_ref):
-    p = jnp.dot(w_ref[...], b_ref[...], preferred_element_type=F32)
+def contract_hi(w_ref, b_ref):
+    p = jnp.dot(w_ref[...], b_ref[0:PTS, :], preferred_element_type=F32)
     return p[:16] + p[16:32] + p[32:]
+
+
+def contract_lo(w_ref, b_ref):
+    p = jnp.dot(w_ref[0:32, :], b_ref[PTS : 2 * PTS, :], preferred_element_type=F32)
+    return p[:16] + p[16:]
 
 
 def combine(acc, x, n, reg_sq):
@@ -281,10 +285,12 @@
     b = (b0, b1)
 
     def block(i):
-        return jnp.where(i == 0, FAR0, jnp.where(i < PEERS, i - 1, i))
+        late = jnp.where(i < 47, i, jnp.where(i < 55, i + 8, i - 8))
+        far = jnp.where(i == 0, FAR0, jnp.where(i < 15, FAR0 - 7 + i, late))
+        return jnp.where(kind(i) == 1, far, jnp.where(i < 15, i - 1, i - 8))
 
     def kind(i):
-        return jnp.where(i == 0, 1, jnp.where(i < PEERS, 0, 1))
+        return jnp.where(i == 0, 1, jnp.where(i < 8, 0, jnp.where(i < 15, 1, jnp.where(i < 39, 0, 1))))
 
     def prep(i, j):
         prepare(big[block(i)], center, row, ya[j % 2], w[j % 4])
@@ -294,11 +300,14 @@
         q = 1 - p
         half = PTS // 2
         xa = xa_ref[kind(i + 1)]
+        before_kind = kind(i - 1)
+        before_w = w[(j - 1) % 4]
+        acc_ref[before_kind] += contract_hi(before_w, b[q])
         if more > 0:
             distances(ya[q], 0, half, xa, d[q])
-        acc_ref[kind(i - 1)] += contract(w[(j - 1) % 4], b[q])
         for r in range(4):
             weights(d[p], CHUNK * r, CHUNK, b[p])
+        acc_ref[before_kind] += contract_lo(before_w, b[q])
         if more > 0:
             distances(ya[q], half, half, xa, d[q])
         for r in range(4, 8):
@@ -313,39 +322,44 @@
     big[0 : NEAR_FIRST - 1] = fine(coarse[0 : NEAR_FIRST - 1])
     prep(1, 1)
 
-    def take_far(f):
-        @pl.when((f > 0) & (lax.rem(f, YN) != 0))
+    def take_far(i):
+        f = block(i) - FAR0
+
+        @pl.when((kind(i) == 1) & (lax.rem(f, YN) != 0))
         def _():
             far_copy(own_ref, 0, f, 0, 1).wait_recv()
 
     def body(k, c):
-        @pl.when(k == 1)
+        @pl.when(k == 2)
         def _():
             far_copy(own_ref, 1, 0, 1, 0).wait_recv()
             far_copy(big.at[FAR0 + YN], 2, 0, 1, 0).start()
             lax.fori_loop(1, YN, fan(1), 0)
             far_copy(own_ref, 3, 0, 3, 0).wait_recv()
             lax.fori_loop(1, YN, fan(3), 0)
+
+        @pl.when(k == 3)
+        def _():
             lax.fori_loop(NEAR_FIRST, PEERS, take_near, 0)
             big[NEAR_FIRST - 1 : FAR0] = fine(coarse[NEAR_FIRST - 1 : FAR0])
 
-        @pl.when(k == 3)
+        @pl.when(k == 5)
         def _():
             far_copy(big.at[FAR0 + YN], 2, 0, 1, 0).wait_recv()
             lax.fori_loop(1, YN, fan(2), 0)
 
         for j in range(4):
-            take_far(4 * k + j + 2 - FAR0)
+            take_far(4 * k + j + 2)
         for j in range(4):
             step(4 * k + j, j)
         return c
 
     lax.fori_loop(0, 15, body, 0)
-    take_far(BLOCKS - 1 - FAR0)
+    take_far(BLOCKS - 1)
     step(BLOCKS - 3, 0)
     step(BLOCKS - 2, 1, more=1)
     step(BLOCKS - 1, 2, more=0)
-    acc_ref[1] += contract(w2, b0)
+    acc_ref[1] += contract_hi(w2, b0) + contract_lo(w2, b0)
 
     near = combine(acc_ref[0], x, n, NEAR_REG_SQ)
     far = combine(acc_ref[1], x, n, FAR_REG_SQ)
@@ -390,7 +404,7 @@
             pltpu.VMEM((2, 16, PTS), F32),
         ]
         + [pltpu.VMEM((48, PTS), BF16)] * 2
-        + [pltpu.VMEM((48, 2 * PTS), BF16)] * 4
+        + [pltpu.VMEM((48, PTS), BF16)] * 4
         + [pltpu.VMEM((PTS, PTS), F32)] * 2
         + [pltpu.VMEM((2 * PTS, PTS), BF16)] * 2
         + [pltpu.SemaphoreType.DMA((5,))]

time: 58.4 us -> 56 us (0.959)
  Pallas kernels: 57 us -> 54.5 us
    pallas_call x1, Pallas kernels: 57 us -> 54.5 us  [shards(): pl.pallas_call(main_kernel, out_shape=jax.ShapeDtypeStruct((3, PTS), F32)...]
where the time goes in v3:
time: 56 us; the launch traced here: 55.8 us
  Pallas kernels  54.5 us (97%)
  local copies, waits for them, and re-layouts  1.3 us (2%)
    pallas_call x1, Pallas kernels, shards(): pl.pallas_call(main_kernel, out_shape=jax.ShapeDtypeStruct((3, PTS), F32)...  54.5 us
    unnamed x1, local copies, waits for them, and re-layouts  1.3 us

profile of v3, /device:TPU:1, one launch (start us, length us, event | category | flops | bytes accessed | tf_op | source)
XLA Modules:
  0.0 55.8 jit_solution(5945594139372752034)
XLA Ops:
  0.0 54.5 %shard_map.55 = f32[3,512]{1,0:T(4,128)} custom-call(f32[3,512]{1,0:T(4,128)} %pos_hbm.1, f32[3,512]{1,0:T(4,128)} %den_hbm.1, f32[32,128]{1,0:T(8,128)} %up_hbm.1, s32[1,32]{1,0:T(1,128)} %map_hbm.1, s32[2,124]{1,0:T(2,128)} %bitcast.3), custom_call_target="tpu_custom_call" | custom-call | tf_op jit(solution)/shard_map/pallas_call | solution.py:384
  54.5 1.3 %copy.7 = f32[3,512]{1,0:T(4,128)} copy(f32[3,512]{1,0:T(4,128)} %shard_map.55) | data formatting | bytes 12288

commit v4 on v3

--- a/solution.py
+++ b/solution.py
@@ -133,33 +133,40 @@
 ):
     blk = lax.axis_index("blk")
     nbr = lax.axis_index("nbr")
-    zh = blk // YN
+    zh = lax.div(blk, YN)
     y = lax.rem(blk, YN)
-    zl = nbr // (2 * XN)
-    xc = lax.rem(nbr // 2, XN)
+    zl = lax.div(nbr, 2 * XN)
+    xc = lax.rem(lax.div(nbr, 2), XN)
     core = lax.rem(nbr, 2)
 
     def column(dz, dy):
         return (lax.rem(zh + dz, ZN) * YN + lax.rem(y + dy, YN), nbr)
 
     def row_index(o):
-        dz = o // (2 * XN)
-        dx = lax.rem(o // 2, XN)
+        dz = lax.div(o, 2 * XN)
+        dx = lax.rem(lax.div(o, 2), XN)
         dc = lax.rem(o, 2)
         return (lax.rem(zl + dz, ZN) * XN + lax.rem(xc + dx, XN)) * 2 + lax.rem(core + dc, 2)
 
     def far_copy(src, dz, dy, hop_z, hop_y):
         f = dz * YN + dy
         return pltpu.make_async_remote_copy(
-            src_ref=src, dst_ref=big.at[FAR0 + f], send_sem=far_send.at[f], recv_sem=far_recv.at[f],
+            src_ref=src, dst_ref=big.at[FAR0 + f], send_sem=far_send, recv_sem=far_recv.at[f],
             device_id=column(hop_z, hop_y), device_id_type=MESH,
         )
 
-    def near_copy(o):
+    def near_copy(o, group):
         return pltpu.make_async_remote_copy(
             src_ref=tiles.at[o], dst_ref=coarse.at[o - 1],
-            send_sem=near_send.at[o - 1], recv_sem=near_recv.at[o - 1],
+            send_sem=near_send, recv_sem=near_recv.at[group],
             device_id=(blk, row_index(o)), device_id_type=MESH,
+        )
+
+    def near_all(first, end, group):
+        return pltpu.make_async_remote_copy(
+            src_ref=tiles.at[first:end], dst_ref=coarse.at[first - 1 : end - 1],
+            send_sem=near_send, recv_sem=near_recv.at[group],
+            device_id=(blk, row_index(jnp.int32(1))), device_id_type=MESH,
         )
 
     loads = [
@@ -207,7 +214,9 @@
     for s in range(SLOTS):
         value = jnp.sum(jnp.where((hit > 0.5) & (rank == s), number, 0.0), axis=1, keepdims=True)
         chosen = jnp.where(lane == s, value, chosen)
-    ids_ref[...] = chosen.astype(jnp.int32)
+    k = chosen.astype(jnp.int32) - 1
+    quarter = jnp.bitwise_and(lane - k, 3)
+    ids_ref[...] = jnp.where(k < 0, PANELS, jnp.bitwise_and(k, PANELS - 4) + quarter)
     to_smem = pltpu.make_async_copy(ids_ref, ids_smem, load_sem.at[0])
     to_smem.start()
 
@@ -225,18 +234,46 @@
     lane_slot = lax.broadcasted_iota(jnp.int32, (8, 128), 1) // 32
     to_smem.wait()
 
-    def route(o, c):
+    def route(o):
         peer = row_index(o)
         tile = jnp.zeros((8, 128), F32)
         for s in range(SLOTS):
-            k = jnp.minimum(jnp.maximum(ids_smem[peer, s] - 1, -1), PANELS - 1)
-            at = jnp.where(k < 0, PANELS, 4 * (k // 4) + jnp.bitwise_and(s - k, 3))
-            at = jnp.minimum(jnp.maximum(at, 0), PANELS)
+            at = jnp.minimum(jnp.maximum(ids_smem[peer, s], 0), PANELS)
             tile = jnp.where(lane_slot == s, table[at], tile)
         tiles[o] = tile
+
+    def route_four(i, c):
+        for u in range(4):
+            route(4 * i + u)
         return c
 
-    lax.fori_loop(1, PEERS, route, 0)
+    lax.fori_loop(0, PEERS // 4, route_four, 0)
+
+    pl.semaphore_wait(barrier, 2 + (YN - 1) + (PEERS - 1))
+    far_copy(own_ref, 1, 0, 1, 0).start()
+    far_copy(own_ref, 3, 0, 3, 0).start()
+
+    def send_near(group):
+        def send(o, c):
+            near_copy(o, group).start()
+            return c
+
+        return send
+
+    def send_own(o, c):
+        far_copy(own_ref, 0, o, 0, o).start()
+        return c
+
+    def fan(dz):
+        def send(o, c):
+            far_copy(big.at[FAR0 + dz * YN], dz, o, 0, o).start()
+            return c
+
+        return send
+
+    lax.fori_loop(1, NEAR_FIRST, send_near(0), 0)
+    lax.fori_loop(1, YN, send_own, 0)
+    lax.fori_loop(NEAR_FIRST, PEERS, send_near(1), 0)
 
     up = up_ref[...]
     none = jnp.zeros_like(up)
@@ -252,32 +289,6 @@
     b1[...] = jnp.zeros_like(b1)
     w3[...] = jnp.zeros_like(w3)
     row = lax.broadcasted_iota(jnp.int32, (8, PTS), 0)
-
-    pl.semaphore_wait(barrier, 2 + (YN - 1) + (PEERS - 1))
-    far_copy(own_ref, 1, 0, 1, 0).start()
-    far_copy(own_ref, 3, 0, 3, 0).start()
-
-    def send_near(o, c):
-        near_copy(o).start()
-        return c
-
-    def send_own(o, c):
-        far_copy(own_ref, 0, o, 0, o).start()
-        return c
-
-    def take_near(o, c):
-        near_copy(o).wait_recv()
-        return c
-
-    def fan(dz):
-        def send(o, c):
-            far_copy(big.at[FAR0 + dz * YN], dz, o, 0, o).start()
-            return c
-
-        return send
-
-    lax.fori_loop(1, PEERS, send_near, 0)
-    lax.fori_loop(1, YN, send_own, 0)
 
     ya = (ya0, ya1)
     w = (w0, w1, w2, w3)
@@ -317,7 +328,7 @@
 
     prep(0, 0)
     distances(ya0, 0, PTS, xa_ref[1], d0)
-    lax.fori_loop(1, NEAR_FIRST, take_near, 0)
+    near_all(1, NEAR_FIRST, 0).wait_recv()
     fine = functools.partial(upsampled, up=split3(wide[...]))
     big[0 : NEAR_FIRST - 1] = fine(coarse[0 : NEAR_FIRST - 1])
     prep(1, 1)
@@ -340,7 +351,7 @@
 
         @pl.when(k == 3)
         def _():
-            lax.fori_loop(NEAR_FIRST, PEERS, take_near, 0)
+            near_all(NEAR_FIRST, PEERS, 1).wait_recv()
             big[NEAR_FIRST - 1 : FAR0] = fine(coarse[NEAR_FIRST - 1 : FAR0])
 
         @pl.when(k == 5)
@@ -366,16 +377,12 @@
     for a in range(3):
         out_ref[a : a + 1, :] = STOKES_COEF * (far[a] + near[a])
 
-    def sent_near(o, c):
-        near_copy(o).wait_send()
-        return c
-
-    def sent_far(f, c):
-        far_copy(own_ref, 0, f, 0, 1).wait_send()
-        return c
-
-    lax.fori_loop(1, PEERS, sent_near, 0)
-    lax.fori_loop(1, COLUMN, sent_far, 0)
+    near_all(1, PEERS, 0).wait_send()
+    pltpu.make_async_remote_copy(
+        src_ref=big.at[FAR0 + 1 : BLOCKS], dst_ref=big.at[FAR0 + 1 : BLOCKS],
+        send_sem=far_send, recv_sem=far_recv.at[0],
+        device_id=column(1, 0), device_id_type=MESH,
+    ).wait_send()
 
 
 def shards(positions, density, upsample, cell_map, near_list):
@@ -408,8 +415,8 @@
         + [pltpu.VMEM((PTS, PTS), F32)] * 2
         + [pltpu.VMEM((2 * PTS, PTS), BF16)] * 2
         + [pltpu.SemaphoreType.DMA((5,))]
-        + [pltpu.SemaphoreType.DMA((PEERS - 1,))] * 2
-        + [pltpu.SemaphoreType.DMA((COLUMN,))] * 2,
+        + [pltpu.SemaphoreType.DMA, pltpu.SemaphoreType.DMA((2,))]
+        + [pltpu.SemaphoreType.DMA, pltpu.SemaphoreType.DMA((COLUMN,))],
         compiler_params=pltpu.CompilerParams(
             collective_id=0, has_side_effects=True, vmem_limit_bytes=62 << 20
         ),

time: 56 us -> 54.6 us (0.975)
  Pallas kernels: 54.5 us -> 53.1 us
    pallas_call x1, Pallas kernels: 54.5 us -> 53.1 us  [shards(): pl.pallas_call(main_kernel, out_shape=jax.ShapeDtypeStruct((3, PTS), F32)...]
where the time goes in v4:
time: 54.6 us; the launch traced here: 54.4 us
  Pallas kernels  53.1 us (97%)
  local copies, waits for them, and re-layouts  1.3 us (2%)
    pallas_call x1, Pallas kernels, shards(): pl.pallas_call(main_kernel, out_shape=jax.ShapeDtypeStruct((3, PTS), F32)...  53.1 us
    unnamed x1, local copies, waits for them, and re-layouts  1.3 us

profile of v4, /device:TPU:1, one launch (start us, length us, event | category | flops | bytes accessed | tf_op | source)
XLA Modules:
  0.0 54.4 jit_solution(3270583834372601557)
XLA Ops:
  0.0 53.1 %shard_map.55 = f32[3,512]{1,0:T(4,128)} custom-call(f32[3,512]{1,0:T(4,128)} %pos_hbm.1, f32[3,512]{1,0:T(4,128)} %den_hbm.1, f32[32,128]{1,0:T(8,128)} %up_hbm.1, s32[1,32]{1,0:T(1,128)} %map_hbm.1, s32[2,124]{1,0:T(2,128)} %bitcast.3), custom_call_target="tpu_custom_call" | custom-call | tf_op jit(solution)/shard_map/pallas_call | solution.py:391
  53.1 1.3 %copy.7 = f32[3,512]{1,0:T(4,128)} copy(f32[3,512]{1,0:T(4,128)} %shard_map.55) | data formatting | bytes 12288

commit v5 on v4

--- a/solution.py
+++ b/solution.py
@@ -129,7 +129,7 @@
     pos_hbm, den_hbm, up_hbm, map_hbm, list_hbm, out_ref,
     pos_ref, den_ref, up_ref, map_ref, list_ref, ids_ref, ids_smem, table, tiles, wide,
     own_ref, coarse, big, xa_ref, acc_ref, ya0, ya1, w0, w1, w2, w3, d0, d1, b0, b1,
-    load_sem, near_send, near_recv, far_send, far_recv,
+    load_sem, near_send, near_recv, far_send, far_recv, fan_recv,
 ):
     blk = lax.axis_index("blk")
     nbr = lax.axis_index("nbr")
@@ -151,8 +151,16 @@
     def far_copy(src, dz, dy, hop_z, hop_y):
         f = dz * YN + dy
         return pltpu.make_async_remote_copy(
-            src_ref=src, dst_ref=big.at[FAR0 + f], send_sem=far_send, recv_sem=far_recv.at[f],
+            src_ref=src, dst_ref=big.at[FAR0 + f], send_sem=far_send,
+            recv_sem=fan_recv.at[dz] if hop_z == 0 else far_recv.at[dz],
             device_id=column(hop_z, hop_y), device_id_type=MESH,
+        )
+
+    def fan_all(dz):
+        blocks = big.at[FAR0 + dz * YN + 1 : FAR0 + dz * YN + YN]
+        return pltpu.make_async_remote_copy(
+            src_ref=blocks, dst_ref=blocks, send_sem=far_send, recv_sem=fan_recv.at[dz],
+            device_id=column(0, 1), device_id_type=MESH,
         )
 
     def near_copy(o, group):
@@ -333,14 +341,11 @@
     big[0 : NEAR_FIRST - 1] = fine(coarse[0 : NEAR_FIRST - 1])
     prep(1, 1)
 
-    def take_far(i):
-        f = block(i) - FAR0
-
-        @pl.when((kind(i) == 1) & (lax.rem(f, YN) != 0))
-        def _():
-            far_copy(own_ref, 0, f, 0, 1).wait_recv()
-
-    def body(k, c):
+    def first_body(k, c):
+        @pl.when(k == 1)
+        def _():
+            fan_all(0).wait_recv()
+
         @pl.when(k == 2)
         def _():
             far_copy(own_ref, 1, 0, 1, 0).wait_recv()
@@ -349,24 +354,36 @@
             far_copy(own_ref, 3, 0, 3, 0).wait_recv()
             lax.fori_loop(1, YN, fan(3), 0)
 
-        @pl.when(k == 3)
+        for j in range(4):
+            step(4 * k + j, j)
+        return c
+
+    def body(k, c):
+        @pl.when(k == 0)
         def _():
             near_all(NEAR_FIRST, PEERS, 1).wait_recv()
             big[NEAR_FIRST - 1 : FAR0] = fine(coarse[NEAR_FIRST - 1 : FAR0])
 
-        @pl.when(k == 5)
+        @pl.when(k == 1)
         def _():
             far_copy(big.at[FAR0 + YN], 2, 0, 1, 0).wait_recv()
             lax.fori_loop(1, YN, fan(2), 0)
 
-        for j in range(4):
-            take_far(4 * k + j + 2)
-        for j in range(4):
-            step(4 * k + j, j)
-        return c
-
-    lax.fori_loop(0, 15, body, 0)
-    take_far(BLOCKS - 1)
+        @pl.when(k == 2)
+        def _():
+            fan_all(1).wait_recv()
+            fan_all(3).wait_recv()
+
+        @pl.when(k == 3)
+        def _():
+            fan_all(2).wait_recv()
+
+        for j in range(12):
+            step(12 * k + 12 + j, j % 4)
+        return c
+
+    lax.fori_loop(0, 3, first_body, 0)
+    lax.fori_loop(0, 4, body, 0)
     step(BLOCKS - 3, 0)
     step(BLOCKS - 2, 1, more=1)
     step(BLOCKS - 1, 2, more=0)
@@ -380,7 +397,7 @@
     near_all(1, PEERS, 0).wait_send()
     pltpu.make_async_remote_copy(
         src_ref=big.at[FAR0 + 1 : BLOCKS], dst_ref=big.at[FAR0 + 1 : BLOCKS],
-        send_sem=far_send, recv_sem=far_recv.at[0],
+        send_sem=far_send, recv_sem=far_recv.at[1],
         device_id=column(1, 0), device_id_type=MESH,
     ).wait_send()
 
@@ -416,7 +433,7 @@
         + [pltpu.VMEM((2 * PTS, PTS), BF16)] * 2
         + [pltpu.SemaphoreType.DMA((5,))]
         + [pltpu.SemaphoreType.DMA, pltpu.SemaphoreType.DMA((2,))]
-        + [pltpu.SemaphoreType.DMA, pltpu.SemaphoreType.DMA((COLUMN,))],
+        + [pltpu.SemaphoreType.DMA, pltpu.SemaphoreType.DMA((ZN,)), pltpu.SemaphoreType.DMA((ZN,))],
         compiler_params=pltpu.CompilerParams(
             collective_id=0, has_side_effects=True, vmem_limit_bytes=62 << 20
         ),

time: 54.6 us -> 52.3 us (0.958)
  Pallas kernels: 53.1 us -> 50.8 us
    pallas_call x1, Pallas kernels: 53.1 us -> 50.8 us  [shards(): pl.pallas_call(main_kernel, out_shape=jax.ShapeDtypeStruct((3, PTS), F32)...]
where the time goes in v5:
time: 52.3 us; the launch traced here: 52.1 us
  Pallas kernels  50.8 us (97%)
  local copies, waits for them, and re-layouts  1.3 us (2%)
    pallas_call x1, Pallas kernels, shards(): pl.pallas_call(main_kernel, out_shape=jax.ShapeDtypeStruct((3, PTS), F32)...  50.8 us
    unnamed x1, local copies, waits for them, and re-layouts  1.3 us

profile of v5, /device:TPU:1, one launch (start us, length us, event | category | flops | bytes accessed | tf_op | source)
XLA Modules:
  0.0 52.1 jit_solution(6123291524361216906)
XLA Ops:
  0.0 50.8 %shard_map.55 = f32[3,512]{1,0:T(4,128)} custom-call(f32[3,512]{1,0:T(4,128)} %pos_hbm.1, f32[3,512]{1,0:T(4,128)} %den_hbm.1, f32[32,128]{1,0:T(8,128)} %up_hbm.1, s32[1,32]{1,0:T(1,128)} %map_hbm.1, s32[2,124]{1,0:T(2,128)} %bitcast.3), custom_call_target="tpu_custom_call" | custom-call | tf_op jit(solution)/shard_map/pallas_call | solution.py:408
  50.8 1.3 %copy.7 = f32[3,512]{1,0:T(4,128)} copy(f32[3,512]{1,0:T(4,128)} %shard_map.55) | data formatting | bytes 12288
